TPU v7x, 512 devices: a whole 4x8x8 slice. The times are simulated.
512 devices in a mesh: tx: 16 (over z, core), ty: 8 (over y_hi, x), mode: 4 (over y_lo).
Axes of the slice: x: 4, y: 8 (y_hi: 2, y_lo: 4; y = y_hi * 4 + y_lo), z: 8, core: 2. Of those that a mesh axis runs over, the one named last changes fastest.
Arguments:
- object_field: float32 [2, 2048, 2048], P(None, 'tx', 'ty'), may hold values from -5 to 5
- probe: float32 [2, 8, 256, 256], P(None, 'mode'), may hold values from -1.5 to 1.5
- amplitudes: bfloat16 [16, 8, 2, 256, 256], P('tx', 'ty'), may hold values from 0.29882812 to 2.5
- centers: int32 [16, 8, 2, 2], P('tx', 'ty'), may hold values from 0 to 255, as said below
- live: int32 [16, 8], P('tx', 'ty'), may hold values from 1 to 2, as said below
Outputs:
- updated: float32 [2, 2048, 2048], P(None, 'tx', 'ty')
Inputs may be any that keep to these rules, and one draw needn't show every extreme that they name: `centers`: the first component is under 128, the second under 256; some live slot sits at offsets (127, 255) and some at (0, 0). A tile's positions fill its slots 0 to live - 1; some tile has all 2 slots live and some only one.
All inputs are finite; a program needn't handle non-finite values.
Results may differ from a plain program's by a relative error of at most 0.006.
Values may be sent and summed in bfloat16 or wider, within the bound.
A program may use at most 64 MiB of HBM per device.

v0:
```python
import math

import jax
import jax.numpy as jnp
from jax import lax
from jax.sharding import PartitionSpec as P

power_floor = 0.01
regularizer = 0.1


def padded_2(block, sides, width):
    for axis, dim in sides:
        count = lax.axis_size(axis)
        forward = [(i, i + 1) for i in range(count - 1)]
        backward = [(target, source) for source, target in forward]
        low = lax.ppermute(
            lax.slice_in_dim(block, block.shape[dim] - width, None, axis=dim), axis, forward
        )
        high = lax.ppermute(lax.slice_in_dim(block, 0, width, axis=dim), axis, backward)
        block = jnp.concatenate([low, block, high], axis=dim)
    return block


def dft_tables(pattern_side):
    index_line = jnp.arange(pattern_side, dtype=jnp.int32)
    product_table = index_line[:, None] * index_line[None, :] % pattern_side
    angle_table = product_table.astype(jnp.float32) * (2.0 * math.pi / pattern_side)
    scaling = 1.0 / math.sqrt(pattern_side)
    table_real = (jnp.cos(angle_table) * scaling).astype(jnp.bfloat16)
    table_imaginary = (-jnp.sin(angle_table) * scaling).astype(jnp.bfloat16)
    return (table_real, table_imaginary)


def left_mult(matrix, signal):
    return jnp.einsum("uv,kvw->kuw", matrix, signal, preferred_element_type=jnp.float32)


def right_mult(signal, matrix):
    return jnp.einsum("kuv,vw->kuw", signal, matrix, preferred_element_type=jnp.float32)


def left_apply(matrix_real, matrix_imaginary, signal_real, signal_imaginary):
    return (
        left_mult(matrix_real, signal_real) - left_mult(matrix_imaginary, signal_imaginary),
        left_mult(matrix_real, signal_imaginary) + left_mult(matrix_imaginary, signal_real),
    )


def right_apply(matrix_real, matrix_imaginary, signal_real, signal_imaginary):
    return (
        right_mult(signal_real, matrix_real) - right_mult(signal_imaginary, matrix_imaginary),
        right_mult(signal_real, matrix_imaginary) + right_mult(signal_imaginary, matrix_real),
    )


def forward_wave(patch, probe_real, probe_imaginary, table_real, table_imaginary):
    patch_real = patch[0].astype(jnp.float32)
    patch_imaginary = patch[1].astype(jnp.float32)
    exit_real = (probe_real * patch_real - probe_imaginary * patch_imaginary).astype(jnp.bfloat16)
    exit_imaginary = (probe_real * patch_imaginary + probe_imaginary * patch_real).astype(
        jnp.bfloat16
    )
    half_real, half_imaginary = left_apply(table_real, table_imaginary, exit_real, exit_imaginary)
    far_real, far_imaginary = right_apply(
        table_real,
        table_imaginary,
        half_real.astype(jnp.bfloat16),
        half_imaginary.astype(jnp.bfloat16),
    )
    return (exit_real, exit_imaginary, far_real, far_imaginary)


def backward_wave(
    far_real,
    far_imaginary,
    power,
    amplitude,
    exit_real,
    exit_imaginary,
    probe_real,
    probe_imaginary,
    table_real,
    table_imaginary,
):
    factor = amplitude.astype(jnp.float32) / jnp.sqrt(power + power_floor)
    fixed_real = (far_real * factor).astype(jnp.bfloat16)
    fixed_imaginary = (far_imaginary * factor).astype(jnp.bfloat16)
    back_half_real, back_half_imaginary = left_apply(
        table_real, -table_imaginary, fixed_real, fixed_imaginary
    )
    back_real, back_imaginary = right_apply(
        table_real,
        -table_imaginary,
        back_half_real.astype(jnp.bfloat16),
        back_half_imaginary.astype(jnp.bfloat16),
    )
    diff_real = back_real - exit_real.astype(jnp.float32)
    diff_imaginary = back_imaginary - exit_imaginary.astype(jnp.float32)
    grad_real = jnp.sum(probe_real * diff_real + probe_imaginary * diff_imaginary, axis=0)
    grad_imaginary = jnp.sum(probe_real * diff_imaginary - probe_imaginary * diff_real, axis=0)
    return (grad_real, grad_imaginary)


def on_device(object_field, probe, amplitudes, centers, live):
    pattern_side = probe.shape[2]
    half_width = pattern_side // 2
    tile_rows = object_field.shape[1]
    tile_cols = object_field.shape[2]
    slot_total = centers.shape[2]
    channels = 3
    table_real, table_imaginary = dft_tables(pattern_side)
    object_low = object_field.astype(jnp.bfloat16)
    padded = padded_2(object_low, (("tx", 1), ("ty", 2)), half_width)
    live_count = live[0, 0]
    anchor = jnp.zeros((), jnp.int32)
    extended = jnp.zeros(
        (channels, tile_rows + pattern_side, tile_cols + pattern_side), jnp.float32
    )

    def place_of(slot_index):
        return (centers[0, 0, slot_index, 0], centers[0, 0, slot_index, 1])

    def patch_of(row_at, col_at):
        return lax.dynamic_slice(padded, (anchor, row_at, col_at), (2, pattern_side, pattern_side))

    def deposit(extended, row_at, col_at, grad_real, grad_imaginary, weight):
        block = jnp.stack([grad_real, grad_imaginary, weight])
        current = lax.dynamic_slice(
            extended, (anchor, row_at, col_at), (channels, pattern_side, pattern_side)
        )
        return lax.dynamic_update_slice(extended, current + block, (anchor, row_at, col_at))

    probe_real = probe[0]
    probe_imaginary = probe[1]
    modes_here = probe.shape[1]
    weight = jnp.sum(probe_real * probe_real + probe_imaginary * probe_imaginary, axis=0)
    far_store = jnp.zeros((slot_total, 2, modes_here, pattern_side, pattern_side), jnp.float32)
    exit_store = jnp.zeros((slot_total, 2, modes_here, pattern_side, pattern_side), jnp.bfloat16)
    power_part = jnp.zeros((slot_total, pattern_side, pattern_side), jnp.float32)

    def look(slot_index, state):
        far_store, exit_store, power_part = state
        row_at, col_at = place_of(slot_index)
        exit_real, exit_imaginary, far_real, far_imaginary = forward_wave(
            patch_of(row_at, col_at), probe_real, probe_imaginary, table_real, table_imaginary
        )
        far_store = lax.dynamic_update_index_in_dim(
            far_store, jnp.stack([far_real, far_imaginary]), slot_index, 0
        )
        exit_store = lax.dynamic_update_index_in_dim(
            exit_store, jnp.stack([exit_real, exit_imaginary]), slot_index, 0
        )
        power_slot = jnp.sum(far_real * far_real + far_imaginary * far_imaginary, axis=0)
        power_part = lax.dynamic_update_index_in_dim(power_part, power_slot, slot_index, 0)
        return (far_store, exit_store, power_part)

    far_store, exit_store, power_part = lax.fori_loop(
        0, live_count, look, (far_store, exit_store, power_part)
    )
    power_all = lax.psum(power_part.astype(jnp.bfloat16), "mode").astype(jnp.float32)

    def apply_slot(slot_index, extended):
        row_at, col_at = place_of(slot_index)
        far_slot = lax.dynamic_index_in_dim(far_store, slot_index, 0, keepdims=False)
        exit_slot = lax.dynamic_index_in_dim(exit_store, slot_index, 0, keepdims=False)
        power = lax.dynamic_index_in_dim(power_all, slot_index, 0, keepdims=False)
        amplitude = lax.dynamic_index_in_dim(amplitudes[0, 0], slot_index, 0, keepdims=False)
        grad_real, grad_imaginary = backward_wave(
            far_slot[0],
            far_slot[1],
            power,
            amplitude,
            exit_slot[0],
            exit_slot[1],
            probe_real,
            probe_imaginary,
            table_real,
            table_imaginary,
        )
        return deposit(extended, row_at, col_at, grad_real, grad_imaginary, weight)

    extended = lax.fori_loop(0, live_count, apply_slot, extended)
    rows_out = jnp.concatenate(
        [extended[:, :half_width, :], extended[:, tile_rows + half_width :, :]], axis=1
    )
    rows_back = padded_2(rows_out.astype(jnp.bfloat16), (("tx", 1),), half_width).astype(
        rows_out.dtype
    )
    inner = extended[:, half_width : half_width + tile_rows, :]
    inner = inner.at[:, :half_width, :].add(rows_back[:, :half_width, :])
    inner = inner.at[:, tile_rows - half_width :, :].add(rows_back[:, 3 * half_width :, :])
    cols_out = jnp.concatenate(
        [inner[:, :, :half_width], inner[:, :, tile_cols + half_width :]], axis=2
    )
    cols_back = padded_2(cols_out.astype(jnp.bfloat16), (("ty", 2),), half_width).astype(
        cols_out.dtype
    )
    core = inner[:, :, half_width : half_width + tile_cols]
    core = core.at[:, :, :half_width].add(cols_back[:, :, :half_width])
    core = core.at[:, :, tile_cols - half_width :].add(cols_back[:, :, 3 * half_width :])
    summed = lax.psum(core.astype(jnp.bfloat16), "mode").astype(jnp.float32)
    return object_field + summed[:2] / (summed[2] + regularizer)


def solution(mesh):
    return jax.shard_map(
        on_device,
        mesh=mesh,
        in_specs=(
            P(None, "tx", "ty"),
            P(None, "mode", None, None),
            P("tx", "ty", None, None, None),
            P("tx", "ty", None, None),
            P("tx", "ty"),
        ),
        out_specs=P(None, "tx", "ty"),
        check_vma=False,
    )
```

profile of v0, /device:TPU:6, one launch (start us, length us, event | category | flops | bytes accessed | tf_op | source)
XLA Modules:
  0.0 308.5 jit_solution(16685017725092557172)
XLA Ops:
  6.5 1.2 copy.14
  7.7 1.3 collective-permute-start.1
  9.0 3.0 collective-permute-start
  12.1 0.9 collective-permute-done
  13.1 7.6 %collective-permute-start.2 = (bf16[2,384,128]{1,2,0:T(8,128)(2,1)S(1)}, bf16[2,384,128]{1,2,0:T(8,128)(2,1)S(1)}, u32[]{:S(2)}, u32[]{:S(2)}) collective-permute-start(bf16[2,384,128]{1,2,0:T(8,128)(2,1)S(1)} %get-tuple-element.527), channel_id=1, source_target_pairs={{0,4},{4,8},{8,12},{12,16},{16,20},{20,24},{24,28},{1,5},{5,9},{9,... | collective-permute-start | bytes 589832 | tf_op jit(solution)/shard_map/ppermute | solution.py:17
  20.8 1.9 collective-permute-start.3
  24.7 10.2 %collective-permute-done.3 = bf16[2,384,128]{1,2,0:T(8,128)(2,1)} collective-permute-done((bf16[2,384,128]{1,2,0:T(8,128)(2,1)S(1)}, bf16[2,384,128]{1,2,0:T(8,128)(2,1)}, u32[]{:S(2)}, u32[]{:S(2)}) %collective-permute-start.3) | collective-permute-done | bytes 196640 | tf_op jit(solution)/shard_map/ppermute | solution.py:20
  35.0 1.1 pad_maximum_fusion
  36.8 1.1 broadcast_in_dim.35
  37.9 1.5 broadcast_in_dim.34
  39.4 20.1 %while.36 = (s32[]{:T(128)}, f32[2,2,2,256,256]{4,3,2,1,0:T(8,128)}, bf16[2,2,2,256,256]{3,4,2,1,0:T(8,128)(2,1)}, bf16[2,256,256]{1,2,0:T(8,128)(2,1)}, s32[]{:...) while((s32[]{:T(128)}, ...), condition=%wide.region_2.3_spmd.clone.clone, body=%wide.region_0.2_spmd.clone.clone.sunk | while | flops 550305792 | bytes 17170740 | solution.py:158
  45.1 1.2 fusion.240
  46.3 1.2 fusion.241
  47.5 1.2 fusion.243
  48.7 1.2 fusion.244
  49.8 1.2 fusion.245
  51.0 1.2 fusion.242
  52.2 1.2 convolution_subtract_fusion.5
  53.4 1.9 add_reduce_fusion.5
  55.3 1.0 copy.45
  57.8 1.1 fusion.246
  59.6 2.0 add_reduce_fusion.2
  61.7 77.3 %all-reduce.3.cloned.1.call-done = bf16[2,256,256]{1,2,0:T(8,128)(2,1)} async-done(((bf16[2,256,256]{1,2,0:T(8,128)(2,1)}), bf16[2,256,256]{1,2,0:T(8,128)(2,1)}) %all-reduce.3.cloned.1.call-update) | async-done | bytes 262160 | tf_op jit(solution)/shard_map/psum | solution.py:161
  139.0 1.8 convert_element_type.192
  141.1 40.8 %while.37 = (s32[]{:T(128)}, f32[3,384,512]{2,1,0:T(8,128)S(1)}, s32[]{:T(128)}, s32[1,1,2,2]{3,2,1,0:T(2,128)S(1)}, f32[2,2,2,256,256]{4,3,2,1,0:T(8,128)}, /*i...) while((s32[]{:T(128)}, f32[3,384,512]{2,1,0:T(8,128)S(1)}, ...), condition=%wide.region_8.9_spmd.clone.clone, body=%wide.region_5.8_spmd.clone.clone.sunk | while | flops 550371328 | bytes 32899572 | solution.py:183
  146.3 0.9 constant_dynamic-slice_fusion.16
  147.4 1.7 fusion.264
  149.1 1.1 constant_dynamic-slice_fusion.17
  151.8 1.3 constant_dynamic-slice_fusion.15
  153.1 1.0 copy.46
  154.3 2.2 fusion.268
  156.5 2.3 fusion.269
  158.8 1.2 fusion.265
  160.0 1.2 fusion.266
  161.2 1.2 fusion.271
  162.5 1.2 fusion.267
  163.7 1.2 fusion.270
  164.9 1.3 add_reduce_fusion.6
  166.2 1.2 maximum_add_fusion.2
  167.4 13.8 %dynamic_update_slice.35 = f32[3,384,512]{2,1,0:T(8,128)S(1)} dynamic-update-slice(f32[3,384,512]{2,1,0:T(8,128)S(1)} %get-tuple-element.752, f32[3,256,256]{2,1,0:T(8,128)S(1)} %maximum_add_fusion.2, s32[]{:T(128)} %constant.211.clone.1..sunk.1, s32[]{:T(128)S(6)} %select_n.188, s32[]{:T(128)S(6)} %select_n.189) | dynamic-update-slice | bytes 1572868 | tf_op jit(solution)/shard_map/while/body/dynamic_update_slice | solution.py:132
  182.1 1.3 collective-permute-start.4
  183.4 1.3 collective-permute-start.5
  184.7 40.1 %collective-permute-done.5 = bf16[3,128,512]{2,1,0:T(8,128)(2,1)S(1)} collective-permute-done((bf16[3,128,512]{2,1,0:T(8,128)(2,1)S(1)}, bf16[3,128,512]{2,1,0:T(8,128)(2,1)S(1)}, u32[]{:S(2)}, u32[]{:S(2)}) %collective-permute-start.5) | collective-permute-done | bytes 393248 | tf_op jit(solution)/shard_map/ppermute | solution.py:20
  225.0 2.1 collective-permute-start.6
  227.1 3.9 %collective-permute-start.7 = (bf16[3,128,128]{2,1,0:T(8,128)(2,1)S(1)}, bf16[3,128,128]{2,1,0:T(8,128)(2,1)S(1)}, u32[]{:S(2)}, u32[]{:S(2)}) collective-permute-start(bf16[3,128,128]{2,1,0:T(8,128)(2,1)S(1)} %get-tuple-element.526), channel_id=1, source_target_pairs={{4,0},{8,4},{12,8},{16,12},{20,16},{24,20},{28,24},{5,1},{9,5},{13... | collective-permute-start | bytes 294920 | tf_op jit(solution)/shard_map/ppermute | solution.py:20
  231.7 8.0 %collective-permute-done.7 = bf16[3,128,128]{2,1,0:T(8,128)(2,1)S(1)} collective-permute-done((bf16[3,128,128]{2,1,0:T(8,128)(2,1)S(1)}, bf16[3,128,128]{2,1,0:T(8,128)(2,1)S(1)}, u32[]{:S(2)}, u32[]{:S(2)}) %collective-permute-start.7) | collective-permute-done | bytes 98336 | tf_op jit(solution)/shard_map/ppermute | solution.py:20
  240.5 59.5 %all-reduce.5.cloned.1.call-done = bf16[3,128,256]{2,1,0:T(8,128)(2,1)} async-done(((bf16[3,128,256]{2,1,0:T(8,128)(2,1)}), bf16[3,128,256]{2,1,0:T(8,128)(2,1)}) %all-reduce.5.cloned.1.call-update) | async-done | bytes 196624 | tf_op jit(solution)/shard_map/psum | solution.py:202
  300.0 1.0 convert_element_type.196
  (68 shorter events, 10.9 us)
Async XLA Ops:
  6.5 16.2 %copy-start.8 = (f32[2,2,256,256]{3,2,1,0:T(8,128)S(1)}, f32[2,2,256,256]{3,2,1,0:T(8,128)}, u32[]{:S(2)}) copy-start(f32[2,2,256,256]{3,2,1,0:T(8,128)} %param.22) | copy-start | bytes 3145732
  6.5 132.4 %all-reduce.3.cloned.1.call-start = ((), (), s32[]{:S(2)}) async-start(), calls=%async_computation | async-start | bytes 524288 | tf_op jit(solution)/shard_map/psum | solution.py:161
  7.7 4.3 %collective-permute-start.1 = (bf16[2,128,256]{1,2,0:T(8,128)(2,1)S(1)}, bf16[2,128,256]{1,2,0:T(8,128)(2,1)S(1)}, u32[]{:S(2)}, u32[]{:S(2)}) collective-permute-start(bf16[2,128,256]{1,2,0:T(8,128)(2,1)S(1)} %copy.14), channel_id=1, source_target_pairs={{32,0},{64,32},{96,64},{128,96},{160,128},{192,160},{224,192},{256... | collective-permute-start | bytes 393224 | tf_op jit(solution)/shard_map/ppermute | solution.py:20
  9.0 4.0 %collective-permute-start = (bf16[2,128,256]{1,2,0:T(8,128)(2,1)S(1)}, bf16[2,128,256]{1,2,0:T(8,128)(2,1)S(1)}, u32[]{:S(2)}, u32[]{:S(2)}) collective-permute-start(bf16[2,128,256]{1,2,0:T(8,128)(2,1)S(1)} %copy.14), channel_id=1, source_target_pairs={{0,32},{32,64},{64,96},{96,128},{128,160},{160,192},{192,224},{224... | collective-permute-start | bytes 393224 | tf_op jit(solution)/shard_map/ppermute | solution.py:17
  12.1 10.7 %copy-start.10 = (bf16[2,128,256]{1,2,0:T(8,128)(2,1)}, bf16[2,128,256]{1,2,0:T(8,128)(2,1)S(1)}, u32[]{:S(2)}) copy-start(bf16[2,128,256]{1,2,0:T(8,128)(2,1)S(1)} %collective-permute-done.1) | copy-start | bytes 393220
  13.0 9.8 %copy-start.12 = (bf16[2,128,256]{1,2,0:T(8,128)(2,1)}, bf16[2,128,256]{1,2,0:T(8,128)(2,1)S(1)}, u32[]{:S(2)}) copy-start(bf16[2,128,256]{1,2,0:T(8,128)(2,1)S(1)} %collective-permute-done) | copy-start | bytes 393220
  13.1 10.9 %collective-permute-start.2 = (bf16[2,384,128]{1,2,0:T(8,128)(2,1)S(1)}, bf16[2,384,128]{1,2,0:T(8,128)(2,1)S(1)}, u32[]{:S(2)}, u32[]{:S(2)}) collective-permute-start(bf16[2,384,128]{1,2,0:T(8,128)(2,1)S(1)} %get-tuple-element.527), channel_id=1, source_target_pairs={{0,4},{4,8},{8,12},{12,16},{16,20},{20,24},{24,28},{1,5},{5,9},{9,... | collective-permute-start | bytes 589832 | tf_op jit(solution)/shard_map/ppermute | solution.py:17
  20.8 14.2 %collective-permute-start.3 = (bf16[2,384,128]{1,2,0:T(8,128)(2,1)S(1)}, bf16[2,384,128]{1,2,0:T(8,128)(2,1)}, u32[]{:S(2)}, u32[]{:S(2)}) collective-permute-start(bf16[2,384,128]{1,2,0:T(8,128)(2,1)S(1)} %get-tuple-element.528), channel_id=1, source_target_pairs={{4,0},{8,4},{12,8},{16,12},{20,16},{24,20},{28,24},{5,1},{9,5},{13... | collective-permute-start | bytes 589832 | tf_op jit(solution)/shard_map/ppermute | solution.py:20
  22.8 0.8 copy-start.1
  22.8 15.0 %copy-start.3 = (f32[2,256,256]{2,1,0:T(8,128)}, f32[2,256,256]{2,1,0:T(8,128)S(1)}, u32[]{:S(2)}) copy-start(f32[2,256,256]{2,1,0:T(8,128)S(1)} %get-tuple-element.742) | copy-start | bytes 1572868
  22.8 12.1 %copy-start.11 = (bf16[2,128,256]{1,2,0:T(8,128)(2,1)S(1)}, bf16[2,128,256]{1,2,0:T(8,128)(2,1)}, u32[]{:S(2)}) copy-start(bf16[2,128,256]{1,2,0:T(8,128)(2,1)} %copy-done.10) | copy-start | bytes 393220
  22.9 12.1 %copy-start.13 = (bf16[2,128,256]{1,2,0:T(8,128)(2,1)S(1)}, bf16[2,128,256]{1,2,0:T(8,128)(2,1)}, u32[]{:S(2)}) copy-start(bf16[2,128,256]{1,2,0:T(8,128)(2,1)} %copy-done.12) | copy-start | bytes 393220
  24.1 0.7 copy-start.14
  36.1 3.3 %copy-start.15 = (s32[1,1,2,2]{3,2,1,0:T(2,128)S(1)}, s32[1,1,2,2]{3,2,1,0:T(2,128)}, u32[]{:S(2)}) copy-start(s32[1,1,2,2]{3,2,1,0:T(2,128)} %param.24) | copy-start | bytes 52
  59.6 240.4 %all-reduce.5.cloned.1.call-start = ((), (), s32[]{:S(2)}) async-start(), calls=%async_computation.1 | async-start | bytes 393216 | tf_op jit(solution)/shard_map/psum | solution.py:202
  154.3 4.5 %copy-start.5 = (f32[1,1,2,256,256]{3,4,2,1,0:T(8,128)S(1)}, f32[1,1,2,256,256]{3,4,2,1,0:T(8,128)}, u32[]{:S(2)}) copy-start(f32[1,1,2,256,256]{3,4,2,1,0:T(8,128)} %copy.46) | copy-start | bytes 1572868 | tf_op jit(solution)/shard_map/while
  154.3 4.5 %copy-start.7 = (f32[256,256]{0,1:T(8,128)S(1)}, f32[256,256]{0,1:T(8,128)}, u32[]{:S(2)}) copy-start(f32[256,256]{0,1:T(8,128)} %fusion.264) | copy-start | bytes 786436 | tf_op jit(solution)/shard_map/while
  160.0 3.6 %copy-start.6 = (bf16[1,1,2,256,256]{4,3,2,1,0:T(8,128)(2,1)S(1)}, bf16[1,1,2,256,256]{4,3,2,1,0:T(8,128)(2,1)}, u32[]{:S(2)}) copy-start(bf16[1,1,2,256,256]{4,3,2,1,0:T(8,128)(2,1)} %copy.49) | copy-start | bytes 786436 | tf_op jit(solution)/shard_map/while
  162.4 2.4 copy-start
  162.4 2.4 copy-start.2
  162.5 2.4 copy-start.4
  182.1 2.6 collective-permute-start.4
  183.4 41.4 %collective-permute-start.5 = (bf16[3,128,512]{2,1,0:T(8,128)(2,1)S(1)}, bf16[3,128,512]{2,1,0:T(8,128)(2,1)S(1)}, u32[]{:S(2)}, u32[]{:S(2)}) collective-permute-start(bf16[3,128,512]{2,1,0:T(8,128)(2,1)S(1)} %get-tuple-element.522), channel_id=1, source_target_pairs={{32,0},{64,32},{96,64},{128,96},{160,128},{192,160},{224,192},{256... | collective-permute-start | bytes 1179656 | tf_op jit(solution)/shard_map/ppermute | solution.py:20
  225.0 75.9 %copy-start.9 = (f32[2,128,256]{2,1,0:T(8,128)S(1)}, f32[2,128,256]{2,1,0:T(8,128)}, u32[]{:S(2)}) copy-start(f32[2,128,256]{2,1,0:T(8,128)} %param.21) | copy-start | bytes 786436
  225.0 6.6 %collective-permute-start.6 = (bf16[3,128,128]{2,1,0:T(8,128)(2,1)S(1)}, bf16[3,128,128]{2,1,0:T(8,128)(2,1)S(1)}, u32[]{:S(2)}, u32[]{:S(2)}) collective-permute-start(bf16[3,128,128]{2,1,0:T(8,128)(2,1)S(1)} %get-tuple-element.525), channel_id=1, source_target_pairs={{0,4},{4,8},{8,12},{12,16},{16,20},{20,24},{24,28},{1,5},{5,9},{9,... | collective-permute-start | bytes 294920 | tf_op jit(solution)/shard_map/ppermute | solution.py:17
  227.1 12.5 %collective-permute-start.7 = (bf16[3,128,128]{2,1,0:T(8,128)(2,1)S(1)}, bf16[3,128,128]{2,1,0:T(8,128)(2,1)S(1)}, u32[]{:S(2)}, u32[]{:S(2)}) collective-permute-start(bf16[3,128,128]{2,1,0:T(8,128)(2,1)S(1)} %get-tuple-element.526), channel_id=1, source_target_pairs={{4,0},{8,4},{12,8},{16,12},{20,16},{24,20},{28,24},{5,1},{9,5},{13... | collective-permute-start | bytes 294920 | tf_op jit(solution)/shard_map/ppermute | solution.py:20
Sparse Core Ops, SparseCore 0:
  59.7 79.2 all-reduce.2
  240.6 59.3 all-reduce.4
where the time goes:
time: 307 us; the launch traced here: 309 us
  waiting for transfers between devices  197 us (64%)
  local copies, waits for them, and re-layouts  29.5 us (10%)
  starting transfers between devices  22.5 us (7%)
  matrix products  21.9 us (7%)
  between operations  13.7 us (4%)
  other arithmetic  13.1 us (4%)
  loops' own time  10.8 us (4%)
    psum x1, waiting for transfers between devices, on_device(): lax.psum(power_part.astype(jnp.bfloat16), 'mode').astype(jnp.float32)  77.3 us
    psum x1, waiting for transfers between devices, on_device(): summed = lax.psum(core.astype(jnp.bfloat16), 'mode').astype(jnp.float32)  59.5 us
    ppermute x4, waiting for transfers between devices, padded_2(): lax.ppermute(lax.slice_in_dim(block, 0, width, axis=dim), axis, backward)  58.3 us
    ppermute x4, starting transfers between devices, padded_2(): lax.ppermute(lax.slice_in_dim(block, block.shape[dim] - width, None, axis...  14.1 us
    dynamic_update_slice x1, local copies, waits for them, and re-layouts, deposit(): lax.dynamic_update_slice(extended, current + block, (anchor, row_at, col_...  13.8 us
    dot_general x8, matrix products, left_mult(): jnp.einsum('uv,kvw->kuw', matrix, signal, preferred_element_type=jnp.floa...  11.6 us
    dot_general x8, matrix products, right_mult(): jnp.einsum('kuv,vw->kuw', signal, matrix, preferred_element_type=jnp.floa...  10.3 us
    ppermute x4, starting transfers between devices, padded_2(): lax.ppermute(lax.slice_in_dim(block, 0, width, axis=dim), axis, backward)  8.43 us
  transfers between devices with their start and end apart: 10, of which 8 were waited for; matrix products, arithmetic and copies ran while one was open for 1% of the time, Pallas kernels for 0%

commit v1 on v0

v1 whole, which is shorter than its diff:
```python
import math

import jax
import jax.numpy as jnp
import numpy as np
from jax import lax
from jax.experimental import pallas as pl
from jax.experimental.pallas import tpu as pltpu
from jax.sharding import PartitionSpec as P

power_floor = 0.01
regularizer = 0.1
W = 256
HW = 128
TR = 128
TC = 256
Q = 32
f32 = jnp.float32
bf16 = jnp.bfloat16
i32 = jnp.int32
MESH = pl.DeviceIdType.MESH


def dft_tables():
    line = np.arange(W)
    angle = ((line[:, None] * line[None, :]) % W).astype(np.float32) * np.float32(2.0 * math.pi / W)
    scaling = np.float32(1.0 / math.sqrt(W))
    return jnp.asarray(
        np.stack([np.cos(angle) * scaling, -np.sin(angle) * scaling]).astype(np.float32)
    ).astype(bf16)


def dot(a, b):
    return jnp.dot(a, b, preferred_element_type=f32)


def one_hot(cond):
    return jnp.where(cond, 1.0, 0.0).astype(bf16)


def iota(shape, dim):
    return lax.broadcasted_iota(i32, shape, dim)


def kernel(
    obj_hbm,
    probe_hbm,
    amp_hbm,
    table_hbm,
    centers_ref,
    live_ref,
    out_ref,
    obj_v,
    probe_v,
    amp_v,
    tab,
    pb,
    pad,
    ib,
    mat_a,
    mat_b,
    mat_bc,
    mat_d,
    sel_p,
    sel_s,
    sel_pt,
    sel_st,
    patch,
    x_s,
    h_s,
    far_s,
    pow_s,
    wt,
    fix_s,
    r_s,
    back_s,
    grad,
    ext,
    zrecv,
    xsend,
    xrecv,
    mid,
    core_s,
    rs_s,
    rs_r,
    ag_s,
    wq,
    local_sem,
    send,
    recv,
):
    tx, ty, m = lax.axis_index("tx"), lax.axis_index("ty"), lax.axis_index("mode")
    nx, ny, nm = lax.axis_size("tx"), lax.axis_size("ty"), lax.axis_size("mode")
    half_ny = ny // 2
    c = lax.rem(tx, 2)
    slot = m // 2
    part = lax.rem(m, 2)

    def at(tx_at, ty_at, m_at):
        return (tx_at, ty_at, m_at)

    right_ty = lax.rem(ty + 1, ny)
    left_ty = lax.rem(ty + ny - 1, ny)
    right_m = jnp.where(lax.rem(ty, half_ny) == half_ny - 1, nm - 1 - m, m)
    left_m = jnp.where(lax.rem(ty, half_ny) == 0, nm - 1 - m, m)
    right = at(tx, right_ty, right_m)
    left = at(tx, left_ty, left_m)
    up = at(lax.rem(tx + nx - 1, nx), ty, m)
    down = at(lax.rem(tx + 1, nx), ty, m)
    partner = at(tx + 1 - 2 * c, ty, m)
    far_ty = lax.rem(ty + half_ny, ny)
    ring_up = at(tx, jnp.where(m == nm - 1, far_ty, ty), lax.rem(m + 1, nm))
    ring_down = at(tx, jnp.where(m == 0, far_ty, ty), lax.rem(m + nm - 1, nm))
    mates = [at(tx, ty, lax.rem(m + d, nm)) for d in (1, 2, 3)]

    def remote(index, src, dst, to):
        return pltpu.make_async_remote_copy(
            src_ref=src,
            dst_ref=dst,
            send_sem=send.at[index],
            recv_sem=recv.at[index],
            device_id=to,
            device_id_type=MESH,
        )

    started = []

    def go(index, src, dst, to):
        copy = remote(index, src, dst, to)
        copy.start()
        started.append(copy)
        return copy

    loads = [
        pltpu.make_async_copy(obj_hbm, obj_v, local_sem.at[0]),
        pltpu.make_async_copy(probe_hbm, probe_v, local_sem.at[1]),
        pltpu.make_async_copy(table_hbm, tab, local_sem.at[2]),
        pltpu.make_async_copy(amp_hbm.at[0, 0], amp_v, local_sem.at[3]),
    ]
    for load in loads:
        load.start()

    barrier = pltpu.get_barrier_semaphore()
    meets = [left, right, up, down, ring_up, ring_down, *mates]
    for to in meets:
        pl.semaphore_signal(barrier, inc=1, device_id=to, device_id_type=MESH)

    row = iota((8, 128), 0)
    ints = jnp.zeros((8, 128), i32)
    for at_row, value in enumerate(
        [
            centers_ref[0, 0, 0, 0],
            centers_ref[0, 0, 0, 1],
            centers_ref[0, 0, 1, 0],
            centers_ref[0, 0, 1, 1],
            live_ref[0, 0],
        ]
    ):
        ints = jnp.where(row == at_row, value, ints)
    ib[1, 1] = ints

    loads[0].wait()
    for p in range(2):
        pad[p, HW : HW + TR, HW : HW + TC] = obj_v[p].astype(bf16)
    pl.semaphore_wait(barrier, len(meets))

    mid_rows = pl.ds(HW, TR)
    top_rows = pl.ds(0, HW)
    low_rows = pl.ds(HW + TR, HW)
    mid_cols = pl.ds(HW, TC)
    left_cols = pl.ds(0, HW)
    right_cols = pl.ds(HW + TC, HW)
    to_left = go(0, pad.at[:, mid_rows, pl.ds(HW, HW)], pad.at[:, mid_rows, right_cols], left)
    to_right = go(1, pad.at[:, mid_rows, pl.ds(TC, HW)], pad.at[:, mid_rows, left_cols], right)
    ints_left = go(2, ib.at[1, 1], ib.at[1, 2], left)
    ints_right = go(3, ib.at[1, 1], ib.at[1, 0], right)
    z_up = go(4, pad.at[:, mid_rows, mid_cols], pad.at[:, low_rows, mid_cols], up)
    z_down = go(5, pad.at[:, mid_rows, mid_cols], pad.at[:, top_rows, mid_cols], down)

    loads[1].wait()
    for p in range(2):
        pb[0, 0, p] = probe_v[p, c].astype(bf16)
    ring = {}
    ring[3, 0] = go(12, pb.at[0, 0, 0], pb.at[3, 0, 0], ring_up)
    ring[1, 1] = go(13, pb.at[0, 0, 1], pb.at[1, 0, 1], ring_down)
    ring[3, 1] = go(14, pb.at[0, 0, 1], pb.at[3, 0, 1], ring_up)
    ring[1, 0] = go(15, pb.at[0, 0, 0], pb.at[1, 0, 0], ring_down)
    for p in range(2):
        pb[0, 1, p] = probe_v[p, 1 - c].astype(bf16)

    loads[2].wait()
    fr, fi = tab[0], tab[1]
    rows_here = pl.ds(pl.multiple_of(part * HW, HW), HW)
    fr_half, fi_half = tab[0, rows_here, :], tab[1, rows_here, :]
    mat_a[0:HW, 0:W] = fr_half
    mat_a[0:HW, W : 2 * W] = -fi_half
    mat_a[HW:W, 0:W] = fi_half
    mat_a[HW:W, W : 2 * W] = fr_half
    mat_b[0:W, 0:W] = fr
    mat_b[0:W, W : 2 * W] = fi
    mat_b[W : 2 * W, 0:W] = -fi
    mat_b[W : 2 * W, W : 2 * W] = fr
    mat_bc[0:W, 0:W] = fr
    mat_bc[0:W, W : 2 * W] = -fi
    mat_bc[W : 2 * W, 0:W] = fi
    mat_bc[W : 2 * W, W : 2 * W] = fr
    cols_here = pl.ds(pl.multiple_of(part * HW, HW), HW)
    fr_cols, fi_cols = tab[0, :, cols_here], tab[1, :, cols_here]
    mat_d[0:W, 0:HW] = fr_cols
    mat_d[0:W, HW:W] = fi_cols
    mat_d[W : 2 * W, 0:HW] = -fi_cols
    mat_d[W : 2 * W, HW:W] = fr_cols

    row_at = jnp.where(slot == 0, centers_ref[0, 0, 0, 0], centers_ref[0, 0, 1, 0])
    col_at = jnp.where(slot == 0, centers_ref[0, 0, 0, 1], centers_ref[0, 0, 1, 1])
    row_from = jnp.where(tx == 0, HW, 0)
    row_to = jnp.where(tx == nx - 1, HW + TR, TR + W)
    col_from = jnp.where(ty == 0, HW, 0)
    col_to = jnp.where(ty == ny - 1, HW + TC, TC + W)

    def selection(shape, outer, base, start, stop):
        big, small = iota(shape, outer), iota(shape, 1 - outer)
        return one_hot((big == small + base) & (big >= start) & (big < stop))

    sel_p[...] = selection((W, TR + W), 1, row_at, row_from, row_to)
    sel_pt[...] = selection((TR + W, W), 0, row_at, row_from, row_to)
    sel_s[...] = selection((TC + W, W), 0, col_at, col_from, col_to)
    sel_st[...] = selection((W, TC + W), 1, col_at, col_from, col_to)

    side = {}

    def pass_on(index, d, p):
        side[d, p] = go(index, pb.at[d, 0, p], pb.at[d, 1, p], partner)

    ring[3, 0].wait_recv()
    ring[2, 0] = go(16, pb.at[3, 0, 0], pb.at[2, 0, 0], ring_up)
    ring[1, 1].wait_recv()
    ring[2, 1] = go(17, pb.at[1, 0, 1], pb.at[2, 0, 1], ring_down)
    pass_on(18, 3, 0)
    pass_on(19, 1, 1)

    to_left.wait_recv()
    to_right.wait_recv()
    z_sides = [
        go(6, pad.at[:, mid_rows, left_cols], pad.at[:, low_rows, left_cols], up),
        go(7, pad.at[:, mid_rows, right_cols], pad.at[:, low_rows, right_cols], up),
        go(8, pad.at[:, mid_rows, left_cols], pad.at[:, top_rows, left_cols], down),
        go(9, pad.at[:, mid_rows, right_cols], pad.at[:, top_rows, right_cols], down),
    ]
    ints_left.wait_recv()
    ints_right.wait_recv()
    ints_up = go(10, ib.at[1], ib.at[2], up)
    ints_down = go(11, ib.at[1], ib.at[0], down)

    ring[3, 1].wait_recv()
    pass_on(20, 3, 1)
    ring[1, 0].wait_recv()
    pass_on(21, 1, 0)

    z_up.wait_recv()
    z_down.wait_recv()
    for copy in z_sides:
        copy.wait_recv()
    for p in range(2):
        shifted = dot(sel_p[...], pad[p]).astype(bf16)
        patch[p] = dot(shifted, sel_s[...])

    ring[2, 0].wait_recv()
    pass_on(22, 2, 0)
    ring[2, 1].wait_recv()
    pass_on(23, 2, 1)

    chunk = 32

    def forward(d, first):
        def exits(i, carry):
            at_rows = pl.ds(pl.multiple_of(i * chunk, chunk), chunk)
            low_rows_at = pl.ds(pl.multiple_of(W + i * chunk, chunk), chunk)
            o_r, o_i = patch[0, at_rows, :], patch[1, at_rows, :]
            weight = jnp.zeros((chunk, W), f32) if first else wt[at_rows, :]
            for j in range(2):
                p_r = pb[d, j, 0, at_rows, :].astype(f32)
                p_i = pb[d, j, 1, at_rows, :].astype(f32)
                x_s[j, at_rows, :] = (p_r * o_r - p_i * o_i).astype(bf16)
                x_s[j, low_rows_at, :] = (p_r * o_i + p_i * o_r).astype(bf16)
                weight = weight + (p_r * p_r + p_i * p_i)
            wt[at_rows, :] = weight
            return carry

        lax.fori_loop(0, W // chunk, exits, 0)
        for j in range(2):
            half = dot(mat_a[...], x_s[j]).astype(bf16)
            h_s[j * HW : (j + 1) * HW, 0:W] = half[0:HW]
            h_s[j * HW : (j + 1) * HW, W : 2 * W] = half[HW:W]
        far_s[d] = dot(h_s[...], mat_b[...])

        def powers(i, carry):
            at_rows = pl.ds(pl.multiple_of(i * chunk, chunk), chunk)
            next_rows = pl.ds(pl.multiple_of(HW + i * chunk, chunk), chunk)
            total = jnp.zeros((chunk, W), f32) if first else pow_s[at_rows, :]
            for rows in (at_rows, next_rows):
                a, b = far_s[d, rows, 0:W], far_s[d, rows, W : 2 * W]
                total = total + (a * a + b * b)
            pow_s[at_rows, :] = total
            return carry

        lax.fori_loop(0, HW // chunk, powers, 0)

    forward(0, True)
    side[3, 0].wait_recv()
    side[3, 1].wait_recv()
    forward(3, False)
    side[1, 1].wait_recv()
    side[1, 0].wait_recv()
    forward(1, False)
    side[2, 0].wait_recv()
    side[2, 1].wait_recv()
    forward(2, False)

    loads[3].wait()
    amplitude = amp_v[slot, rows_here, :].astype(f32)
    pow_s[...] = amplitude / jnp.sqrt(pow_s[...] + power_floor)

    def backward(d, carry):
        def fixes(i, carry):
            at_rows = pl.ds(pl.multiple_of(i * chunk, chunk), chunk)
            next_rows = pl.ds(pl.multiple_of(HW + i * chunk, chunk), chunk)
            factor = pow_s[at_rows, :]
            for rows in (at_rows, next_rows):
                fix_s[rows, 0:W] = (far_s[d, rows, 0:W] * factor).astype(bf16)
                fix_s[rows, W : 2 * W] = (far_s[d, rows, W : 2 * W] * factor).astype(bf16)
            return carry

        lax.fori_loop(0, HW // chunk, fixes, 0)
        half = dot(fix_s[...], mat_bc[...]).astype(bf16)
        for j in range(2):
            r_s[j, 0:HW, :] = half[j * HW : (j + 1) * HW, 0:W]
            r_s[j, HW:W, :] = half[j * HW : (j + 1) * HW, W : 2 * W]
        for j in range(2):
            back_s[j] = dot(mat_d[...], r_s[j])

        def grads(i, carry):
            at_rows = pl.ds(pl.multiple_of(i * chunk, chunk), chunk)
            low_rows_at = pl.ds(pl.multiple_of(W + i * chunk, chunk), chunk)
            g_r, g_i = grad[0, at_rows, :], grad[1, at_rows, :]
            for j in range(2):
                p_r = pb[d, j, 0, at_rows, :].astype(f32)
                p_i = pb[d, j, 1, at_rows, :].astype(f32)
                b_r, b_i = back_s[j, at_rows, :], back_s[j, low_rows_at, :]
                g_r = g_r + (p_r * b_r + p_i * b_i)
                g_i = g_i + (p_r * b_i - p_i * b_r)
            grad[0, at_rows, :] = g_r
            grad[1, at_rows, :] = g_i
            return carry

        lax.fori_loop(0, W // chunk, grads, 0)
        return carry

    for p in range(2):
        grad[p] = -0.5 * wt[...] * patch[p]
    lax.fori_loop(0, 4, backward, 0)

    counts = slot < live_ref[0, 0]
    for p in range(2):
        low = jnp.where(counts, grad[p], 0.0).astype(bf16)
        wide = dot(low, sel_st[...]).astype(bf16)
        ext[p] = dot(sel_pt[...], wide).astype(bf16)

    fold_up = go(24, ext.at[:, top_rows, :], zrecv.at[0], up)
    fold_down = go(25, ext.at[:, low_rows, :], zrecv.at[1], down)

    ints_up.wait_recv()
    ints_down.wait_recv()
    total = jnp.zeros((Q, TC), f32)
    low_weight = wt[...].astype(bf16)
    for a in range(3):
        for b in range(3):
            inside = (
                jnp.where(tx + (a - 1) >= 0, 1, 0)
                * jnp.where(tx + (a - 1) < nx, 1, 0)
                * jnp.where(ty + (b - 1) >= 0, 1, 0)
                * jnp.where(ty + (b - 1) < ny, 1, 0)
            )
            block = ib[a, b]
            alive = block[4:5, 0:1] * inside
            for s in range(2):
                row_of = m * Q + HW - HW * (a - 1) - block[2 * s : 2 * s + 1, 0:1]
                col_of = HW - TC * (b - 1) - block[2 * s + 1 : 2 * s + 2, 0:1]
                pick = one_hot(
                    (iota((Q, W), 1) == iota((Q, W), 0) + row_of) & (alive > s)
                )
                place = one_hot(iota((W, TC), 0) == iota((W, TC), 1) + col_of)
                picked = dot(pick, low_weight).astype(bf16)
                total = total + dot(picked, place)
    wq[...] = total

    fold_up.wait_recv()
    fold_down.wait_recv()
    for p in range(2):
        mid[p] = (
            ext[p, HW : HW + TR, :].astype(f32)
            + zrecv[0, p].astype(f32)
            + zrecv[1, p].astype(f32)
        )
        xsend[0, p] = mid[p, :, 0:HW].astype(bf16)
        xsend[1, p] = mid[p, :, HW + TC :].astype(bf16)
    cols_left = go(26, xsend.at[0], xrecv.at[1], left)
    cols_right = go(27, xsend.at[1], xrecv.at[0], right)
    cols_left.wait_recv()
    cols_right.wait_recv()
    for q in range(4):
        rows = slice(q * Q, (q + 1) * Q)
        for p in range(2):
            core_s[q, p, :, 0:HW] = mid[p, rows, HW : 2 * HW] + xrecv[0, p, rows, :].astype(f32)
            core_s[q, p, :, HW:TC] = mid[p, rows, 2 * HW : 3 * HW] + xrecv[1, p, rows, :].astype(f32)
            rs_s[q, p] = core_s[q, p].astype(bf16)
    sums = []
    for d in (1, 2, 3):
        sums.append(go(27 + d, rs_s.at[lax.rem(m + d, nm)], rs_r.at[d - 1], mates[d - 1]))
    total = core_s[m]
    for d in (1, 2, 3):
        sums[d - 1].wait_recv()
        total = total + rs_r[d - 1].astype(f32)
    scale = wq[...] + regularizer
    for p in range(2):
        ag_s[m, p] = (total[p] / scale).astype(bf16)
    gathers = [go(30 + d, ag_s.at[m], ag_s.at[m], mates[d - 1]) for d in (1, 2, 3)]
    for d in (1, 2, 3):
        gathers[d - 1].wait_recv()
    for q in range(4):
        for p in range(2):
            out_ref[p, q * Q : (q + 1) * Q, :] = ag_s[q, p]
    for copy in started:
        copy.wait_send()


def on_device(object_field, probe, amplitudes, centers, live):
    any_space = pl.BlockSpec(memory_space=pl.ANY)
    smem = pl.BlockSpec(memory_space=pltpu.SMEM)
    vmem = pltpu.VMEM
    update = pl.pallas_call(
        kernel,
        out_shape=jax.ShapeDtypeStruct((2, TR, TC), bf16),
        in_specs=[any_space] * 4 + [smem] * 2,
        out_specs=pl.BlockSpec(memory_space=pltpu.VMEM),
        scratch_shapes=[
            vmem((2, TR, TC), f32),
            vmem((2, 2, W, W), f32),
            vmem((2, W, W), bf16),
            vmem((2, W, W), bf16),
            vmem((4, 2, 2, W, W), bf16),
            vmem((2, TR + W, TC + W), bf16),
            vmem((3, 3, 8, 128), i32),
            vmem((W, 2 * W), bf16),
            vmem((2 * W, 2 * W), bf16),
            vmem((2 * W, 2 * W), bf16),
            vmem((2 * W, W), bf16),
            vmem((W, TR + W), bf16),
            vmem((TC + W, W), bf16),
            vmem((TR + W, W), bf16),
            vmem((W, TC + W), bf16),
            vmem((2, W, W), f32),
            vmem((2, 2 * W, W), bf16),
            vmem((W, 2 * W), bf16),
            vmem((4, W, 2 * W), f32),
            vmem((HW, W), f32),
            vmem((W, W), f32),
            vmem((W, 2 * W), bf16),
            vmem((2, W, W), bf16),
            vmem((2, 2 * W, W), f32),
            vmem((2, W, W), f32),
            vmem((2, TR + W, TC + W), bf16),
            vmem((2, 2, HW, TC + W), bf16),
            vmem((2, 2, TR, HW), bf16),
            vmem((2, 2, TR, HW), bf16),
            vmem((2, TR, TC + W), f32),
            vmem((4, 2, Q, TC), f32),
            vmem((4, 2, Q, TC), bf16),
            vmem((3, 2, Q, TC), bf16),
            vmem((4, 2, Q, TC), bf16),
            vmem((Q, TC), f32),
            pltpu.SemaphoreType.DMA((4,)),
            pltpu.SemaphoreType.DMA((34,)),
            pltpu.SemaphoreType.DMA((34,)),
        ],
        compiler_params=pltpu.CompilerParams(
            collective_id=0, has_side_effects=True, vmem_limit_bytes=56 * 1024 * 1024
        ),
        name="object_update",
    )(object_field, probe, amplitudes, dft_tables(), centers, live)
    return object_field + update.astype(f32)


def solution(mesh):
    return jax.shard_map(
        on_device,
        mesh=mesh,
        in_specs=(
            P(None, "tx", "ty"),
            P(None, "mode", None, None),
            P("tx", "ty", None, None, None),
            P("tx", "ty", None, None),
            P("tx", "ty"),
        ),
        out_specs=P(None, "tx", "ty"),
        check_vma=False,
    )
```

time: 307 us -> 57.1 us (0.19)
  waiting for transfers between devices: 197 us -> 0 us
  Pallas kernels: 0 us -> 54.6 us
  local copies, waits for them, and re-layouts: 29.5 us -> 0.01 us
  starting transfers between devices: 22.5 us -> 0 us
  matrix products: 21.9 us -> 0 us
  between operations: 13.7 us -> 0.68 us
  other arithmetic: 13.1 us -> 1.63 us
  loops' own time: 10.8 us -> 0 us
    psum x2 -> x0, waiting for transfers between devices: 137 us -> none  [the longest x1 77.3 us: on_device(): lax.psum(power_part.astype(jnp.bfloat16), 'mode').astype(jnp.float32)]
    ppermute x8 -> x0, waiting for transfers between devices: 60.1 us -> none  [the longest x4 58.3 us: padded_2(): lax.ppermute(lax.slice_in_dim(block, 0, width, axis=dim), axis, backward)]
    pallas_call x0 -> x1, Pallas kernels: none -> 54.6 us  [on_device(): pl.pallas_call(kernel, out_shape=jax.ShapeDtypeStruct((2, TR, TC), bf16),...]
    ppermute x8 -> x0, starting transfers between devices: 22.5 us -> none  [the longest x4 14.1 us: padded_2(): lax.ppermute(lax.slice_in_dim(block, block.shape[dim] - width, None, axis...]
    dot_general x16 -> x0, matrix products: 21.9 us -> none  [the longest x8 11.6 us: left_mult(): jnp.einsum('uv,kvw->kuw', matrix, signal, preferred_element_type=jnp.floa...]
    dynamic_update_slice x3 -> x0, local copies, waits for them, and re-layouts: 15.4 us -> none  [the longest x1 13.8 us: deposit(): lax.dynamic_update_slice(extended, current + block, (anchor, row_at, col_...]
    another operation x2 -> x0, loops' own time: 10.8 us -> none  [the longest x1 5.52 us: on_device(): extended = lax.fori_loop(0, live_count, apply_slot, extended)]
    convert_element_type x5 -> x0, other arithmetic: 3.73 us -> none  [the longest x1 1.8 us: on_device(): lax.psum(power_part.astype(jnp.bfloat16), 'mode').astype(jnp.float32)]
  transfers between devices with their start and end apart: 10 -> 0, of which waited for: 8 -> 0; matrix products, arithmetic and copies ran while one was open for 1% -> 0% of each run, Pallas kernels for 0% -> 0%
where the time goes in v1:
time: 57.1 us; the launch traced here: 56.9 us
  Pallas kernels  54.6 us (96%)
  other arithmetic  1.63 us (3%)
  between operations  0.68 us (1%)
    pallas_call x1, Pallas kernels, on_device(): pl.pallas_call(kernel, out_shape=jax.ShapeDtypeStruct((2, TR, TC), bf16),...  54.6 us
    add x1, other arithmetic, on_device(): return object_field + update.astype(f32)  1.63 us

profile of v1, /device:TPU:6, one launch (start us, length us, event | category | flops | bytes accessed | tf_op | source)
XLA Modules:
  0.0 56.9 jit_solution(17800954458474678070)
XLA Ops:
  0.7 0.0 copy-start
  0.7 54.6 %object_update.1 = bf16[2,128,256]{2,1,0:T(8,128)(2,1)} custom-call(f32[2,128,256]{2,1,0:T(8,128)} %obj_hbm.1, f32[2,2,256,256]{3,2,1,0:T(8,128)} %probe_hbm.1, bf16[1,1,2,256,256]{4,3,2,1,0:T(8,128)(2,1)} %amp_hbm.1, bf16[2,256,256]{2,1,0:T(8,128)(2,1)} %constant.7.table_hbm, s32[1,1,2,2]{3,2,1,0:T(2,128)} %centers_ref.1, s32[1,1]{1,0:T(1,128)S(6)} %copy.7.live_ref), custom_call_target="tpu_custom_call" | custom-call | tf_op jit(solution)/shard_map/object_update/pallas_call | solution.py:441
  55.3 0.0 copy-done
  55.3 1.6 %convert_add_fusion = f32[2,128,256]{2,1,0:T(8,128)} fusion(f32[2,128,256]{2,1,0:T(8,128)S(1)} %copy-done, bf16[2,128,256]{2,1,0:T(8,128)(2,1)} %object_update.1), kind=kLoop, calls=%fused_computation | loop fusion | flops 131072 | bytes 655360 | tf_op jit(solution)/shard_map/add | solution.py:491
Async XLA Ops:
  0.7 54.6 %copy-start = (f32[2,128,256]{2,1,0:T(8,128)S(1)}, f32[2,128,256]{2,1,0:T(8,128)}, u32[]{:S(2)}) copy-start(f32[2,128,256]{2,1,0:T(8,128)} %obj_hbm.1) | copy-start | bytes 786436

commit v2 on v1

--- a/solution.py
+++ b/solution.py
@@ -85,6 +85,8 @@
     rs_r,
     ag_s,
     wq,
+    wt_low,
+    sel_near,
     local_sem,
     send,
     recv,
@@ -232,13 +234,6 @@
     def pass_on(index, d, p):
         side[d, p] = go(index, pb.at[d, 0, p], pb.at[d, 1, p], partner)
 
-    ring[3, 0].wait_recv()
-    ring[2, 0] = go(16, pb.at[3, 0, 0], pb.at[2, 0, 0], ring_up)
-    ring[1, 1].wait_recv()
-    ring[2, 1] = go(17, pb.at[1, 0, 1], pb.at[2, 0, 1], ring_down)
-    pass_on(18, 3, 0)
-    pass_on(19, 1, 1)
-
     to_left.wait_recv()
     to_right.wait_recv()
     z_sides = [
@@ -247,6 +242,13 @@
         go(8, pad.at[:, mid_rows, left_cols], pad.at[:, top_rows, left_cols], down),
         go(9, pad.at[:, mid_rows, right_cols], pad.at[:, top_rows, right_cols], down),
     ]
+    ring[3, 0].wait_recv()
+    ring[2, 0] = go(16, pb.at[3, 0, 0], pb.at[2, 0, 0], ring_up)
+    ring[1, 1].wait_recv()
+    ring[2, 1] = go(17, pb.at[1, 0, 1], pb.at[2, 0, 1], ring_down)
+    pass_on(18, 3, 0)
+    pass_on(19, 1, 1)
+
     ints_left.wait_recv()
     ints_right.wait_recv()
     ints_up = go(10, ib.at[1], ib.at[2], up)
@@ -361,19 +363,19 @@
     lax.fori_loop(0, 4, backward, 0)
 
     counts = slot < live_ref[0, 0]
+    folds = []
     for p in range(2):
         low = jnp.where(counts, grad[p], 0.0).astype(bf16)
-        wide = dot(low, sel_st[...]).astype(bf16)
-        ext[p] = dot(sel_pt[...], wide).astype(bf16)
-
-    fold_up = go(24, ext.at[:, top_rows, :], zrecv.at[0], up)
-    fold_down = go(25, ext.at[:, low_rows, :], zrecv.at[1], down)
-
-    ints_up.wait_recv()
-    ints_down.wait_recv()
-    total = jnp.zeros((Q, TC), f32)
-    low_weight = wt[...].astype(bf16)
-    for a in range(3):
+        ext[p] = dot(sel_pt[...], low).astype(bf16)
+        folds.append(
+            (
+                go(24 + 2 * p, ext.at[p, top_rows, :], zrecv.at[0, p], up),
+                go(25 + 2 * p, ext.at[p, low_rows, :], zrecv.at[1, p], down),
+            )
+        )
+
+    def weight_rows(a):
+        total = jnp.zeros((Q, TC), f32) if a == 0 else wq[...]
         for b in range(3):
             inside = (
                 jnp.where(tx + (a - 1) >= 0, 1, 0)
@@ -386,50 +388,73 @@
             for s in range(2):
                 row_of = m * Q + HW - HW * (a - 1) - block[2 * s : 2 * s + 1, 0:1]
                 col_of = HW - TC * (b - 1) - block[2 * s + 1 : 2 * s + 2, 0:1]
-                pick = one_hot(
-                    (iota((Q, W), 1) == iota((Q, W), 0) + row_of) & (alive > s)
-                )
+                pick = one_hot((iota((Q, W), 1) == iota((Q, W), 0) + row_of) & (alive > s))
                 place = one_hot(iota((W, TC), 0) == iota((W, TC), 1) + col_of)
-                picked = dot(pick, low_weight).astype(bf16)
+                picked = dot(pick, wt_low[...]).astype(bf16)
                 total = total + dot(picked, place)
-    wq[...] = total
-
-    fold_up.wait_recv()
-    fold_down.wait_recv()
-    for p in range(2):
-        mid[p] = (
-            ext[p, HW : HW + TR, :].astype(f32)
-            + zrecv[0, p].astype(f32)
-            + zrecv[1, p].astype(f32)
+        wq[...] = total
+
+    wt_low[...] = wt[...].astype(bf16)
+    ints_up.wait_recv()
+    ints_down.wait_recv()
+    for index, a in ((0, 2), (1, 0)):
+        block = ib[a, 1]
+        col_there = jnp.where(slot == 0, block[1:2, 0:1], block[3:4, 0:1])
+        sel_near[index] = selection((W, TC + W), 1, col_there, col_from, col_to)
+    for p in range(2):
+        mid[p] = dot(ext[p, HW : HW + TR, :], sel_st[...])
+
+    columns = []
+    for p in range(2):
+        for copy in folds[p]:
+            copy.wait_recv()
+        mid[p] = mid[p] + (
+            dot(zrecv[0, p], sel_near[0]) + dot(zrecv[1, p], sel_near[1])
         )
-        xsend[0, p] = mid[p, :, 0:HW].astype(bf16)
-        xsend[1, p] = mid[p, :, HW + TC :].astype(bf16)
-    cols_left = go(26, xsend.at[0], xrecv.at[1], left)
-    cols_right = go(27, xsend.at[1], xrecv.at[0], right)
-    cols_left.wait_recv()
-    cols_right.wait_recv()
-    for q in range(4):
-        rows = slice(q * Q, (q + 1) * Q)
-        for p in range(2):
-            core_s[q, p, :, 0:HW] = mid[p, rows, HW : 2 * HW] + xrecv[0, p, rows, :].astype(f32)
-            core_s[q, p, :, HW:TC] = mid[p, rows, 2 * HW : 3 * HW] + xrecv[1, p, rows, :].astype(f32)
-            rs_s[q, p] = core_s[q, p].astype(bf16)
+        xsend[p, 0] = mid[p, :, 0:HW].astype(bf16)
+        xsend[p, 1] = mid[p, :, HW + TC :].astype(bf16)
+        columns.append(
+            (
+                go(28 + 2 * p, xsend.at[p, 0], xrecv.at[p, 1], left),
+                go(29 + 2 * p, xsend.at[p, 1], xrecv.at[p, 0], right),
+            )
+        )
+    weight_rows(0)
+    weight_rows(1)
+
     sums = []
-    for d in (1, 2, 3):
-        sums.append(go(27 + d, rs_s.at[lax.rem(m + d, nm)], rs_r.at[d - 1], mates[d - 1]))
-    total = core_s[m]
-    for d in (1, 2, 3):
-        sums[d - 1].wait_recv()
-        total = total + rs_r[d - 1].astype(f32)
+    for p in range(2):
+        for copy in columns[p]:
+            copy.wait_recv()
+        for q in range(4):
+            rows = slice(q * Q, (q + 1) * Q)
+            core_s[p, q, :, 0:HW] = mid[p, rows, HW : 2 * HW] + xrecv[p, 0, rows, :].astype(f32)
+            core_s[p, q, :, HW:TC] = mid[p, rows, 2 * HW : 3 * HW] + xrecv[p, 1, rows, :].astype(f32)
+            rs_s[p, q] = core_s[p, q].astype(bf16)
+        sums.append(
+            [
+                go(31 + 3 * p + d, rs_s.at[p, lax.rem(m + d, nm)], rs_r.at[p, d - 1], mates[d - 1])
+                for d in (1, 2, 3)
+            ]
+        )
+    weight_rows(2)
     scale = wq[...] + regularizer
-    for p in range(2):
-        ag_s[m, p] = (total[p] / scale).astype(bf16)
-    gathers = [go(30 + d, ag_s.at[m], ag_s.at[m], mates[d - 1]) for d in (1, 2, 3)]
-    for d in (1, 2, 3):
-        gathers[d - 1].wait_recv()
-    for q in range(4):
-        for p in range(2):
-            out_ref[p, q * Q : (q + 1) * Q, :] = ag_s[q, p]
+
+    gathers = []
+    for p in range(2):
+        total = core_s[p, m]
+        for d in (1, 2, 3):
+            sums[p][d - 1].wait_recv()
+            total = total + rs_r[p, d - 1].astype(f32)
+        ag_s[p, m] = (total / scale).astype(bf16)
+        gathers.append(
+            [go(37 + 3 * p + d, ag_s.at[p, m], ag_s.at[p, m], mates[d - 1]) for d in (1, 2, 3)]
+        )
+    for p in range(2):
+        for copy in gathers[p]:
+            copy.wait_recv()
+        for q in range(4):
+            out_ref[p, q * Q : (q + 1) * Q, :] = ag_s[p, q]
     for copy in started:
         copy.wait_send()
 
@@ -469,19 +494,21 @@
             vmem((2, W, W), bf16),
             vmem((2, 2 * W, W), f32),
             vmem((2, W, W), f32),
-            vmem((2, TR + W, TC + W), bf16),
-            vmem((2, 2, HW, TC + W), bf16),
+            vmem((2, TR + W, W), bf16),
+            vmem((2, 2, HW, W), bf16),
             vmem((2, 2, TR, HW), bf16),
             vmem((2, 2, TR, HW), bf16),
             vmem((2, TR, TC + W), f32),
-            vmem((4, 2, Q, TC), f32),
-            vmem((4, 2, Q, TC), bf16),
-            vmem((3, 2, Q, TC), bf16),
-            vmem((4, 2, Q, TC), bf16),
+            vmem((2, 4, Q, TC), f32),
+            vmem((2, 4, Q, TC), bf16),
+            vmem((2, 3, Q, TC), bf16),
+            vmem((2, 4, Q, TC), bf16),
             vmem((Q, TC), f32),
+            vmem((W, W), bf16),
+            vmem((2, W, TC + W), bf16),
             pltpu.SemaphoreType.DMA((4,)),
-            pltpu.SemaphoreType.DMA((34,)),
-            pltpu.SemaphoreType.DMA((34,)),
+            pltpu.SemaphoreType.DMA((44,)),
+            pltpu.SemaphoreType.DMA((44,)),
         ],
         compiler_params=pltpu.CompilerParams(
             collective_id=0, has_side_effects=True, vmem_limit_bytes=56 * 1024 * 1024

time: 57.1 us -> 54 us (0.946)
  Pallas kernels: 54.6 us -> 51.5 us
    pallas_call x1, Pallas kernels: 54.6 us -> 51.5 us  [on_device(): pl.pallas_call(kernel, out_shape=jax.ShapeDtypeStruct((2, TR, TC), bf16),...]
where the time goes in v2:
time: 54 us; the launch traced here: 53.8 us
  Pallas kernels  51.5 us (95%)
  other arithmetic  1.63 us (3%)
  between operations  0.68 us (1%)
    pallas_call x1, Pallas kernels, on_device(): pl.pallas_call(kernel, out_shape=jax.ShapeDtypeStruct((2, TR, TC), bf16),...  51.5 us
    add x1, other arithmetic, on_device(): return object_field + update.astype(f32)  1.63 us

profile of v2, /device:TPU:6, one launch (start us, length us, event | category | flops | bytes accessed | tf_op | source)
XLA Modules:
  0.0 53.8 jit_solution(7316204960060864598)
XLA Ops:
  0.7 0.0 copy-start
  0.7 51.5 %object_update.1 = bf16[2,128,256]{2,1,0:T(8,128)(2,1)} custom-call(f32[2,128,256]{2,1,0:T(8,128)} %obj_hbm.1, f32[2,2,256,256]{3,2,1,0:T(8,128)} %probe_hbm.1, bf16[1,1,2,256,256]{4,3,2,1,0:T(8,128)(2,1)} %amp_hbm.1, bf16[2,256,256]{2,1,0:T(8,128)(2,1)} %constant.7.table_hbm, s32[1,1,2,2]{3,2,1,0:T(2,128)} %centers_ref.1, s32[1,1]{1,0:T(1,128)S(6)} %copy.7.live_ref), custom_call_target="tpu_custom_call" | custom-call | tf_op jit(solution)/shard_map/object_update/pallas_call | solution.py:466
  52.1 0.0 copy-done
  52.2 1.6 %convert_add_fusion = f32[2,128,256]{2,1,0:T(8,128)} fusion(f32[2,128,256]{2,1,0:T(8,128)S(1)} %copy-done, bf16[2,128,256]{2,1,0:T(8,128)(2,1)} %object_update.1), kind=kLoop, calls=%fused_computation | loop fusion | flops 131072 | bytes 655360 | tf_op jit(solution)/shard_map/add | solution.py:518
Async XLA Ops:
  0.7 51.5 %copy-start = (f32[2,128,256]{2,1,0:T(8,128)S(1)}, f32[2,128,256]{2,1,0:T(8,128)}, u32[]{:S(2)}) copy-start(f32[2,128,256]{2,1,0:T(8,128)} %obj_hbm.1) | copy-start | bytes 786436

commit v3 on v2

--- a/solution.py
+++ b/solution.py
@@ -47,8 +47,8 @@
     probe_hbm,
     amp_hbm,
     table_hbm,
-    centers_ref,
-    live_ref,
+    centers_hbm,
+    live_hbm,
     out_ref,
     obj_v,
     probe_v,
@@ -87,6 +87,8 @@
     wq,
     wt_low,
     sel_near,
+    centers_ref,
+    live_ref,
     local_sem,
     send,
     recv,
@@ -138,6 +140,8 @@
         pltpu.make_async_copy(probe_hbm, probe_v, local_sem.at[1]),
         pltpu.make_async_copy(table_hbm, tab, local_sem.at[2]),
         pltpu.make_async_copy(amp_hbm.at[0, 0], amp_v, local_sem.at[3]),
+        pltpu.make_async_copy(centers_hbm, centers_ref, local_sem.at[4]),
+        pltpu.make_async_copy(live_hbm, live_ref, local_sem.at[5]),
     ]
     for load in loads:
         load.start()
@@ -147,6 +151,30 @@
     for to in meets:
         pl.semaphore_signal(barrier, inc=1, device_id=to, device_id_type=MESH)
 
+    loads[0].wait()
+    for p in range(2):
+        pad[p, HW : HW + TR, HW : HW + TC] = obj_v[p].astype(bf16)
+    pl.semaphore_wait(barrier, len(meets))
+
+    mid_rows = pl.ds(HW, TR)
+    top_rows = pl.ds(0, HW)
+    low_rows = pl.ds(HW + TR, HW)
+    mid_cols = pl.ds(HW, TC)
+    left_cols = pl.ds(0, HW)
+    right_cols = pl.ds(HW + TC, HW)
+    to_left, to_right = [], []
+    for p in range(2):
+        to_left.append(
+            go(p, pad.at[p, mid_rows, pl.ds(HW, HW)], pad.at[p, mid_rows, right_cols], left)
+        )
+        to_right.append(
+            go(44 + p, pad.at[p, mid_rows, pl.ds(TC, HW)], pad.at[p, mid_rows, left_cols], right)
+        )
+    z_up = go(4, pad.at[:, mid_rows, mid_cols], pad.at[:, low_rows, mid_cols], up)
+    z_down = go(5, pad.at[:, mid_rows, mid_cols], pad.at[:, top_rows, mid_cols], down)
+
+    loads[4].wait()
+    loads[5].wait()
     row = iota((8, 128), 0)
     ints = jnp.zeros((8, 128), i32)
     for at_row, value in enumerate(
@@ -161,23 +189,8 @@
         ints = jnp.where(row == at_row, value, ints)
     ib[1, 1] = ints
 
-    loads[0].wait()
-    for p in range(2):
-        pad[p, HW : HW + TR, HW : HW + TC] = obj_v[p].astype(bf16)
-    pl.semaphore_wait(barrier, len(meets))
-
-    mid_rows = pl.ds(HW, TR)
-    top_rows = pl.ds(0, HW)
-    low_rows = pl.ds(HW + TR, HW)
-    mid_cols = pl.ds(HW, TC)
-    left_cols = pl.ds(0, HW)
-    right_cols = pl.ds(HW + TC, HW)
-    to_left = go(0, pad.at[:, mid_rows, pl.ds(HW, HW)], pad.at[:, mid_rows, right_cols], left)
-    to_right = go(1, pad.at[:, mid_rows, pl.ds(TC, HW)], pad.at[:, mid_rows, left_cols], right)
     ints_left = go(2, ib.at[1, 1], ib.at[1, 2], left)
     ints_right = go(3, ib.at[1, 1], ib.at[1, 0], right)
-    z_up = go(4, pad.at[:, mid_rows, mid_cols], pad.at[:, low_rows, mid_cols], up)
-    z_down = go(5, pad.at[:, mid_rows, mid_cols], pad.at[:, top_rows, mid_cols], down)
 
     loads[1].wait()
     for p in range(2):
@@ -234,14 +247,14 @@
     def pass_on(index, d, p):
         side[d, p] = go(index, pb.at[d, 0, p], pb.at[d, 1, p], partner)
 
-    to_left.wait_recv()
-    to_right.wait_recv()
-    z_sides = [
-        go(6, pad.at[:, mid_rows, left_cols], pad.at[:, low_rows, left_cols], up),
-        go(7, pad.at[:, mid_rows, right_cols], pad.at[:, low_rows, right_cols], up),
-        go(8, pad.at[:, mid_rows, left_cols], pad.at[:, top_rows, left_cols], down),
-        go(9, pad.at[:, mid_rows, right_cols], pad.at[:, top_rows, right_cols], down),
-    ]
+    z_sides = []
+    for p in range(2):
+        to_left[p].wait_recv()
+        to_right[p].wait_recv()
+        for i, cols in enumerate((left_cols, right_cols)):
+            here = pad.at[p, mid_rows, cols]
+            z_sides.append(go(6 + 2 * p + i, here, pad.at[p, low_rows, cols], up))
+            z_sides.append(go(46 + 2 * p + i, here, pad.at[p, top_rows, cols], down))
     ring[3, 0].wait_recv()
     ring[2, 0] = go(16, pb.at[3, 0, 0], pb.at[2, 0, 0], ring_up)
     ring[1, 1].wait_recv()
@@ -461,12 +474,11 @@
 
 def on_device(object_field, probe, amplitudes, centers, live):
     any_space = pl.BlockSpec(memory_space=pl.ANY)
-    smem = pl.BlockSpec(memory_space=pltpu.SMEM)
     vmem = pltpu.VMEM
     update = pl.pallas_call(
         kernel,
-        out_shape=jax.ShapeDtypeStruct((2, TR, TC), bf16),
-        in_specs=[any_space] * 4 + [smem] * 2,
+        out_shape=pltpu.VMEM((2, TR, TC), bf16),
+        in_specs=[any_space] * 6,
         out_specs=pl.BlockSpec(memory_space=pltpu.VMEM),
         scratch_shapes=[
             vmem((2, TR, TC), f32),
@@ -506,9 +518,11 @@
             vmem((Q, TC), f32),
             vmem((W, W), bf16),
             vmem((2, W, TC + W), bf16),
-            pltpu.SemaphoreType.DMA((4,)),
-            pltpu.SemaphoreType.DMA((44,)),
-            pltpu.SemaphoreType.DMA((44,)),
+            pltpu.SMEM((1, 1, 2, 2), i32),
+            pltpu.SMEM((1, 1), i32),
+            pltpu.SemaphoreType.DMA((6,)),
+            pltpu.SemaphoreType.DMA((50,)),
+            pltpu.SemaphoreType.DMA((50,)),
         ],
         compiler_params=pltpu.CompilerParams(
             collective_id=0, has_side_effects=True, vmem_limit_bytes=56 * 1024 * 1024

time: 54 us -> 51.9 us (0.961)
  Pallas kernels: 51.5 us -> 50.4 us
  other arithmetic: 1.63 us -> 0.73 us
    pallas_call x1, Pallas kernels: 51.5 us -> 50.4 us  [on_device(): pl.pallas_call(kernel, out_shape=pltpu.VMEM((2, TR, TC), bf16), in_specs=...]
    add x1, other arithmetic: 1.63 us -> 0.73 us  [on_device(): return object_field + update.astype(f32)]
where the time goes in v3:
time: 51.9 us; the launch traced here: 51.8 us
  Pallas kernels  50.4 us (97%)
  other arithmetic  0.73 us (1%)
  between operations  0.68 us (1%)
    pallas_call x1, Pallas kernels, on_device(): pl.pallas_call(kernel, out_shape=pltpu.VMEM((2, TR, TC), bf16), in_specs=...  50.4 us

profile of v3, /device:TPU:6, one launch (start us, length us, event | category | flops | bytes accessed | tf_op | source)
XLA Modules:
  0.0 51.8 jit_solution(10901572812591948132)
XLA Ops:
  0.7 0.0 copy-start
  0.7 50.4 %object_update.1 = bf16[2,128,256]{2,1,0:T(8,128)(2,1)S(1)} custom-call(f32[2,128,256]{2,1,0:T(8,128)} %obj_hbm.1, f32[2,2,256,256]{3,2,1,0:T(8,128)} %probe_hbm.1, bf16[1,1,2,256,256]{4,3,2,1,0:T(8,128)(2,1)} %amp_hbm.1, bf16[2,256,256]{2,1,0:T(8,128)(2,1)} %constant.7.table_hbm, s32[1,1,2,2]{3,2,1,0:T(2,128)} %centers_hbm.1, s32[1,1]{1,0:T(1,128)S(6)} %copy.7.live_hbm), custom_call_target="tpu_custom_call" | custom-call | tf_op jit(solution)/shard_map/object_update/pallas_call | solution.py:478
  51.0 0.0 copy-done
  51.1 0.7 %convert_add_fusion = f32[2,128,256]{2,1,0:T(8,128)} fusion(f32[2,128,256]{2,1,0:T(8,128)S(1)} %copy-done, bf16[2,128,256]{2,1,0:T(8,128)(2,1)S(1)} %object_update.1), kind=kLoop, calls=%fused_computation | loop fusion | flops 131072 | bytes 655360 | tf_op jit(solution)/shard_map/add | solution.py:532
Async XLA Ops:
  0.7 50.4 %copy-start = (f32[2,128,256]{2,1,0:T(8,128)S(1)}, f32[2,128,256]{2,1,0:T(8,128)}, u32[]{:S(2)}) copy-start(f32[2,128,256]{2,1,0:T(8,128)} %obj_hbm.1) | copy-start | bytes 786436

commit v4 on v3

--- a/solution.py
+++ b/solution.py
@@ -272,6 +272,19 @@
     ring[1, 0].wait_recv()
     pass_on(21, 1, 0)
 
+    chunk = 32
+    for d, js in ((3, (0, 1)), (1, (1, 0))):
+        for j in js:
+            side[d, j].wait_recv()
+    for i in range(W // chunk):
+        at_rows = slice(i * chunk, (i + 1) * chunk)
+        total = jnp.zeros((chunk, W), f32)
+        for d in (0, 3, 1):
+            for j in range(2):
+                p_r = pb[d, j, 0, at_rows, :].astype(f32)
+                p_i = pb[d, j, 1, at_rows, :].astype(f32)
+                total = total + (p_r * p_r + p_i * p_i)
+        wt[at_rows, :] = total
     z_up.wait_recv()
     z_down.wait_recv()
     for copy in z_sides:
@@ -285,95 +298,91 @@
     ring[2, 1].wait_recv()
     pass_on(23, 2, 1)
 
-    chunk = 32
-
-    def forward(d, first):
-        def exits(i, carry):
-            at_rows = pl.ds(pl.multiple_of(i * chunk, chunk), chunk)
-            low_rows_at = pl.ds(pl.multiple_of(W + i * chunk, chunk), chunk)
+    def exits(d, buf, chunks, weigh=False):
+        for i in chunks:
+            at_rows, low_rows_at = slice(i * chunk, (i + 1) * chunk), slice(W + i * chunk, W + (i + 1) * chunk)
             o_r, o_i = patch[0, at_rows, :], patch[1, at_rows, :]
-            weight = jnp.zeros((chunk, W), f32) if first else wt[at_rows, :]
             for j in range(2):
                 p_r = pb[d, j, 0, at_rows, :].astype(f32)
                 p_i = pb[d, j, 1, at_rows, :].astype(f32)
-                x_s[j, at_rows, :] = (p_r * o_r - p_i * o_i).astype(bf16)
-                x_s[j, low_rows_at, :] = (p_r * o_i + p_i * o_r).astype(bf16)
-                weight = weight + (p_r * p_r + p_i * p_i)
-            wt[at_rows, :] = weight
-            return carry
-
-        lax.fori_loop(0, W // chunk, exits, 0)
+                x_s[buf, j, at_rows, :] = (p_r * o_r - p_i * o_i).astype(bf16)
+                x_s[buf, j, low_rows_at, :] = (p_r * o_i + p_i * o_r).astype(bf16)
+                if weigh:
+                    wt[at_rows, :] = wt[at_rows, :] + (p_r * p_r + p_i * p_i)
+
+    def powers(d, first):
+        for i in range(HW // chunk):
+            at_rows = slice(i * chunk, (i + 1) * chunk)
+            total = jnp.zeros((chunk, W), f32) if first else pow_s[at_rows, :]
+            for j in range(2):
+                rows = slice(j * HW + i * chunk, j * HW + (i + 1) * chunk)
+                p, q = far_s[d, rows, 0:W], far_s[d, rows, W : 2 * W]
+                total = total + (p * p + q * q)
+            pow_s[at_rows, :] = total
+
+    def forward(d, buf, then, weigh=False, last=None):
         for j in range(2):
-            half = dot(mat_a[...], x_s[j]).astype(bf16)
+            half = dot(mat_a[...], x_s[buf, j]).astype(bf16)
             h_s[j * HW : (j + 1) * HW, 0:W] = half[0:HW]
             h_s[j * HW : (j + 1) * HW, W : 2 * W] = half[HW:W]
+            if then is not None:
+                exits(then, 1 - buf, range(4 * j, 4 * j + 4), weigh)
         far_s[d] = dot(h_s[...], mat_b[...])
-
-        def powers(i, carry):
-            at_rows = pl.ds(pl.multiple_of(i * chunk, chunk), chunk)
-            next_rows = pl.ds(pl.multiple_of(HW + i * chunk, chunk), chunk)
-            total = jnp.zeros((chunk, W), f32) if first else pow_s[at_rows, :]
-            for rows in (at_rows, next_rows):
-                a, b = far_s[d, rows, 0:W], far_s[d, rows, W : 2 * W]
-                total = total + (a * a + b * b)
-            pow_s[at_rows, :] = total
-            return carry
-
-        lax.fori_loop(0, HW // chunk, powers, 0)
-
-    forward(0, True)
-    side[3, 0].wait_recv()
-    side[3, 1].wait_recv()
-    forward(3, False)
-    side[1, 1].wait_recv()
-    side[1, 0].wait_recv()
-    forward(1, False)
+        if last is not None:
+            powers(last, last == 0)
+
+    exits(0, 0, range(8))
+    forward(0, 0, 3)
+    forward(3, 1, 1, last=0)
     side[2, 0].wait_recv()
     side[2, 1].wait_recv()
-    forward(2, False)
+    forward(1, 0, 2, weigh=True, last=3)
+    forward(2, 1, None, last=1)
+    powers(2, False)
 
     loads[3].wait()
     amplitude = amp_v[slot, rows_here, :].astype(f32)
     pow_s[...] = amplitude / jnp.sqrt(pow_s[...] + power_floor)
 
-    def backward(d, carry):
-        def fixes(i, carry):
-            at_rows = pl.ds(pl.multiple_of(i * chunk, chunk), chunk)
-            next_rows = pl.ds(pl.multiple_of(HW + i * chunk, chunk), chunk)
-            factor = pow_s[at_rows, :]
-            for rows in (at_rows, next_rows):
-                fix_s[rows, 0:W] = (far_s[d, rows, 0:W] * factor).astype(bf16)
-                fix_s[rows, W : 2 * W] = (far_s[d, rows, W : 2 * W] * factor).astype(bf16)
-            return carry
-
-        lax.fori_loop(0, HW // chunk, fixes, 0)
-        half = dot(fix_s[...], mat_bc[...]).astype(bf16)
-        for j in range(2):
-            r_s[j, 0:HW, :] = half[j * HW : (j + 1) * HW, 0:W]
-            r_s[j, HW:W, :] = half[j * HW : (j + 1) * HW, W : 2 * W]
-        for j in range(2):
-            back_s[j] = dot(mat_d[...], r_s[j])
-
-        def grads(i, carry):
-            at_rows = pl.ds(pl.multiple_of(i * chunk, chunk), chunk)
-            low_rows_at = pl.ds(pl.multiple_of(W + i * chunk, chunk), chunk)
+    def fixes(d, buf):
+        for i in range(HW // chunk):
+            factor = pow_s[i * chunk : (i + 1) * chunk, :]
+            for j in range(2):
+                rows = slice(j * HW + i * chunk, j * HW + (i + 1) * chunk)
+                fix_s[buf, rows, 0:W] = (far_s[d, rows, 0:W] * factor).astype(bf16)
+                fix_s[buf, rows, W : 2 * W] = (far_s[d, rows, W : 2 * W] * factor).astype(bf16)
+
+    def grads(d, buf, chunks):
+        for i in chunks:
+            at_rows, low_rows_at = slice(i * chunk, (i + 1) * chunk), slice(W + i * chunk, W + (i + 1) * chunk)
             g_r, g_i = grad[0, at_rows, :], grad[1, at_rows, :]
             for j in range(2):
                 p_r = pb[d, j, 0, at_rows, :].astype(f32)
                 p_i = pb[d, j, 1, at_rows, :].astype(f32)
-                b_r, b_i = back_s[j, at_rows, :], back_s[j, low_rows_at, :]
+                b_r, b_i = back_s[buf, j, at_rows, :], back_s[buf, j, low_rows_at, :]
                 g_r = g_r + (p_r * b_r + p_i * b_i)
                 g_i = g_i + (p_r * b_i - p_i * b_r)
             grad[0, at_rows, :] = g_r
             grad[1, at_rows, :] = g_i
-            return carry
-
-        lax.fori_loop(0, W // chunk, grads, 0)
-        return carry
+
+    def backward(d, buf):
+        half = dot(fix_s[buf], mat_bc[...]).astype(bf16)
+        for j in range(2):
+            r_s[j, 0:HW, :] = half[j * HW : (j + 1) * HW, 0:W]
+            r_s[j, HW:W, :] = half[j * HW : (j + 1) * HW, W : 2 * W]
+        if d < 3:
+            fixes(d + 1, 1 - buf)
+        for j in range(2):
+            if d > 0:
+                grads(d - 1, 1 - buf, range(4 * j, 4 * j + 4))
+            back_s[buf, j] = dot(mat_d[...], r_s[j])
 
     for p in range(2):
         grad[p] = -0.5 * wt[...] * patch[p]
-    lax.fori_loop(0, 4, backward, 0)
+    fixes(0, 0)
+    for d in range(4):
+        backward(d, d % 2)
+    grads(3, 1, range(8))
 
     counts = slot < live_ref[0, 0]
     folds = []
@@ -497,14 +506,14 @@
             vmem((TR + W, W), bf16),
             vmem((W, TC + W), bf16),
             vmem((2, W, W), f32),
-            vmem((2, 2 * W, W), bf16),
+            vmem((2, 2, 2 * W, W), bf16),
             vmem((W, 2 * W), bf16),
             vmem((4, W, 2 * W), f32),
             vmem((HW, W), f32),
             vmem((W, W), f32),
-            vmem((W, 2 * W), bf16),
+            vmem((2, W, 2 * W), bf16),
             vmem((2, W, W), bf16),
-            vmem((2, 2 * W, W), f32),
+            vmem((2, 2, 2 * W, W), f32),
             vmem((2, W, W), f32),
             vmem((2, TR + W, W), bf16),
             vmem((2, 2, HW, W), bf16),

time: 51.9 us -> 51.2 us (0.987)
  Pallas kernels: 50.4 us -> 49.7 us
    pallas_call x1, Pallas kernels: 50.4 us -> 49.7 us  [on_device(): pl.pallas_call(kernel, out_shape=pltpu.VMEM((2, TR, TC), bf16), in_specs=...]
where the time goes in v4:
time: 51.2 us; the launch traced here: 51.1 us
  Pallas kernels  49.7 us (97%)
  other arithmetic  0.73 us (1%)
  between operations  0.68 us (1%)
    pallas_call x1, Pallas kernels, on_device(): pl.pallas_call(kernel, out_shape=pltpu.VMEM((2, TR, TC), bf16), in_specs=...  49.7 us

profile of v4, /device:TPU:6, one launch (start us, length us, event | category | flops | bytes accessed | tf_op | source)
XLA Modules:
  0.0 51.1 jit_solution(17607517767455119571)
XLA Ops:
  0.7 0.0 copy-start
  0.7 49.7 %object_update.1 = bf16[2,128,256]{2,1,0:T(8,128)(2,1)S(1)} custom-call(f32[2,128,256]{2,1,0:T(8,128)} %obj_hbm.1, f32[2,2,256,256]{3,2,1,0:T(8,128)} %probe_hbm.1, bf16[1,1,2,256,256]{4,3,2,1,0:T(8,128)(2,1)} %amp_hbm.1, bf16[2,256,256]{2,1,0:T(8,128)(2,1)} %constant.7.table_hbm, s32[1,1,2,2]{3,2,1,0:T(2,128)} %centers_hbm.1, s32[1,1]{1,0:T(1,128)S(6)} %copy.7.live_hbm), custom_call_target="tpu_custom_call" | custom-call | tf_op jit(solution)/shard_map/object_update/pallas_call | solution.py:487
  50.3 0.0 copy-done
  50.3 0.7 %convert_add_fusion = f32[2,128,256]{2,1,0:T(8,128)} fusion(f32[2,128,256]{2,1,0:T(8,128)S(1)} %copy-done, bf16[2,128,256]{2,1,0:T(8,128)(2,1)S(1)} %object_update.1), kind=kLoop, calls=%fused_computation | loop fusion | flops 131072 | bytes 655360 | tf_op jit(solution)/shard_map/add | solution.py:541
Async XLA Ops:
  0.7 49.7 %copy-start = (f32[2,128,256]{2,1,0:T(8,128)S(1)}, f32[2,128,256]{2,1,0:T(8,128)}, u32[]{:S(2)}) copy-start(f32[2,128,256]{2,1,0:T(8,128)} %obj_hbm.1) | copy-start | bytes 786436

commit v5 on v4

--- a/solution.py
+++ b/solution.py
@@ -87,6 +87,7 @@
     wq,
     wt_low,
     sel_near,
+    cols_s,
     centers_ref,
     live_ref,
     local_sem,
@@ -247,6 +248,10 @@
     def pass_on(index, d, p):
         side[d, p] = go(index, pb.at[d, 0, p], pb.at[d, 1, p], partner)
 
+    ring[3, 0].wait_recv()
+    ring[2, 0] = go(16, pb.at[3, 0, 0], pb.at[2, 0, 0], ring_up)
+    ring[1, 1].wait_recv()
+    ring[2, 1] = go(17, pb.at[1, 0, 1], pb.at[2, 0, 1], ring_down)
     z_sides = []
     for p in range(2):
         to_left[p].wait_recv()
@@ -255,10 +260,6 @@
             here = pad.at[p, mid_rows, cols]
             z_sides.append(go(6 + 2 * p + i, here, pad.at[p, low_rows, cols], up))
             z_sides.append(go(46 + 2 * p + i, here, pad.at[p, top_rows, cols], down))
-    ring[3, 0].wait_recv()
-    ring[2, 0] = go(16, pb.at[3, 0, 0], pb.at[2, 0, 0], ring_up)
-    ring[1, 1].wait_recv()
-    ring[2, 1] = go(17, pb.at[1, 0, 1], pb.at[2, 0, 1], ring_down)
     pass_on(18, 3, 0)
     pass_on(19, 1, 1)
 
@@ -273,25 +274,25 @@
     pass_on(21, 1, 0)
 
     chunk = 32
-    for d, js in ((3, (0, 1)), (1, (1, 0))):
-        for j in js:
-            side[d, j].wait_recv()
     for i in range(W // chunk):
         at_rows = slice(i * chunk, (i + 1) * chunk)
         total = jnp.zeros((chunk, W), f32)
-        for d in (0, 3, 1):
+        for d in (0,):
             for j in range(2):
                 p_r = pb[d, j, 0, at_rows, :].astype(f32)
                 p_i = pb[d, j, 1, at_rows, :].astype(f32)
                 total = total + (p_r * p_r + p_i * p_i)
         wt[at_rows, :] = total
+    for p in range(2):
+        cols_s[p, HW : HW + TR, :] = dot(pad[p, HW : HW + TR, :], sel_s[...]).astype(bf16)
     z_up.wait_recv()
     z_down.wait_recv()
     for copy in z_sides:
         copy.wait_recv()
     for p in range(2):
-        shifted = dot(sel_p[...], pad[p]).astype(bf16)
-        patch[p] = dot(shifted, sel_s[...])
+        for rows in (slice(0, HW), slice(HW + TR, TR + W)):
+            cols_s[p, rows, :] = dot(pad[p, rows, :], sel_s[...]).astype(bf16)
+        patch[p] = dot(sel_p[...], cols_s[p])
 
     ring[2, 0].wait_recv()
     pass_on(22, 2, 0)
@@ -332,8 +333,12 @@
             powers(last, last == 0)
 
     exits(0, 0, range(8))
-    forward(0, 0, 3)
-    forward(3, 1, 1, last=0)
+    side[3, 0].wait_recv()
+    side[3, 1].wait_recv()
+    forward(0, 0, 3, weigh=True)
+    side[1, 1].wait_recv()
+    side[1, 0].wait_recv()
+    forward(3, 1, 1, weigh=True, last=0)
     side[2, 0].wait_recv()
     side[2, 1].wait_recv()
     forward(1, 0, 2, weigh=True, last=3)
@@ -527,6 +532,7 @@
             vmem((Q, TC), f32),
             vmem((W, W), bf16),
             vmem((2, W, TC + W), bf16),
+            vmem((2, TR + W, W), bf16),
             pltpu.SMEM((1, 1, 2, 2), i32),
             pltpu.SMEM((1, 1), i32),
             pltpu.SemaphoreType.DMA((6,)),

time: 51.2 us -> 50.6 us (0.988)
  Pallas kernels: 49.7 us -> 49.1 us
    pallas_call x1, Pallas kernels: 49.7 us -> 49.1 us  [on_device(): pl.pallas_call(kernel, out_shape=pltpu.VMEM((2, TR, TC), bf16), in_specs=...]
where the time goes in v5:
time: 50.6 us; the launch traced here: 50.5 us
  Pallas kernels  49.1 us (97%)
  other arithmetic  0.73 us (1%)
  between operations  0.68 us (1%)
    pallas_call x1, Pallas kernels, on_device(): pl.pallas_call(kernel, out_shape=pltpu.VMEM((2, TR, TC), bf16), in_specs=...  49.1 us

profile of v5, /device:TPU:6, one launch (start us, length us, event | category | flops | bytes accessed | tf_op | source)
XLA Modules:
  0.0 50.5 jit_solution(17217778859499889303)
XLA Ops:
  0.7 0.0 copy-start
  0.7 49.1 %object_update.1 = bf16[2,128,256]{2,1,0:T(8,128)(2,1)S(1)} custom-call(f32[2,128,256]{2,1,0:T(8,128)} %obj_hbm.1, f32[2,2,256,256]{3,2,1,0:T(8,128)} %probe_hbm.1, bf16[1,1,2,256,256]{4,3,2,1,0:T(8,128)(2,1)} %amp_hbm.1, bf16[2,256,256]{2,1,0:T(8,128)(2,1)} %constant.7.table_hbm, s32[1,1,2,2]{3,2,1,0:T(2,128)} %centers_hbm.1, s32[1,1]{1,0:T(1,128)S(6)} %copy.7.live_hbm), custom_call_target="tpu_custom_call" | custom-call | tf_op jit(solution)/shard_map/object_update/pallas_call | solution.py:492
  49.8 0.0 copy-done
  49.8 0.7 %convert_add_fusion = f32[2,128,256]{2,1,0:T(8,128)} fusion(f32[2,128,256]{2,1,0:T(8,128)S(1)} %copy-done, bf16[2,128,256]{2,1,0:T(8,128)(2,1)S(1)} %object_update.1), kind=kLoop, calls=%fused_computation | loop fusion | flops 131072 | bytes 655360 | tf_op jit(solution)/shard_map/add | solution.py:547
Async XLA Ops:
  0.7 49.1 %copy-start = (f32[2,128,256]{2,1,0:T(8,128)S(1)}, f32[2,128,256]{2,1,0:T(8,128)}, u32[]{:S(2)}) copy-start(f32[2,128,256]{2,1,0:T(8,128)} %obj_hbm.1) | copy-start | bytes 786436
